TPU v7x, 32 devices: a whole 2x2x4 slice. The times are simulated.
32 devices in a mesh: dp: 16 (over z, y, x), tensor: 2 (over core).
Axes of the slice: x: 2, y: 2, z: 4, core: 2. Of those that a mesh axis runs over, the one named last changes fastest.
Arguments:
- tokens: bfloat16 [4, 16, 2048, 1024], P(None, 'dp', None, 'tensor'), may hold values from -40 to 40
- routed: int32 [4, 16, 256], P(None, 'dp'), may hold values from 0 to 2047, as said below
- w_query: bfloat16 [1024, 1024], P('dp', 'tensor'), may hold values from -0.1875 to 0.1875
- w_key: bfloat16 [1024, 1024], P('dp', 'tensor'), may hold values from -0.1875 to 0.1875
- w_value: bfloat16 [1024, 1024], P('dp', 'tensor'), may hold values from -0.1875 to 0.1875
- w_out: bfloat16 [1024, 1024], P('tensor', 'dp'), may hold values from -1 to 1
- w_up: bfloat16 [1024, 4096], P('dp', 'tensor'), may hold values from -0.1875 to 0.1875
- w_down: bfloat16 [4096, 1024], P('tensor', 'dp'), may hold values from -0.09375 to 0.09375
- w_route: bfloat16 [1024], P('dp'), may hold values from -0.09375 to 0.09375
- gain_attn: bfloat16 [1024], P('dp'), may hold values from 0.099609375 to 1.8984375
- gain_mlp: bfloat16 [1024], P('dp'), may hold values from 0.099609375 to 1.8984375
- cotangent: bfloat16 [4, 16, 2048, 1024], P(None, 'dp', None, 'tensor'), may hold values from -6 to 6
Outputs:
- output: bfloat16 [4, 16, 2048, 1024], P(None, 'dp', None, 'tensor')
- input_grad: bfloat16 [4, 16, 2048, 1024], P(None, 'dp', None, 'tensor')
- grad_query: float32 [1024, 1024], P('dp', 'tensor')
- grad_key: float32 [1024, 1024], P('dp', 'tensor')
- grad_value: float32 [1024, 1024], P('dp', 'tensor')
- grad_out: float32 [1024, 1024], P('tensor', 'dp')
- grad_up: float32 [1024, 4096], P('dp', 'tensor')
- grad_down: float32 [4096, 1024], P('tensor', 'dp')
- grad_route: float32 [1024], P('dp')
- grad_gain_attn: float32 [1024], P('dp')
- grad_gain_mlp: float32 [1024], P('dp')
Inputs may be any that keep to these rules, and one draw needn't show every extreme that they name: Each row of routed holds 256 different positions of its sequence in rising order.
All inputs are finite; a program needn't handle non-finite values.
Results may differ from a plain program's by a relative error of at most 0.02.
Values may be sent and summed in bfloat16 or wider, within the bound.
A program may use at most 192 MiB of HBM per device.

v0:
```python
import jax
import jax.numpy as jnp
from jax import lax
from jax.sharding import PartitionSpec as P

HD = 64
eps_norm = 1e-05


def rms_norm(values, gain):
    return values * lax.rsqrt(jnp.mean(values * values, -1, keepdims=True) + eps_norm) * gain


def dense(left, right):
    return jnp.dot(left, right, preferred_element_type=jnp.float32)


def shards(
    tokens,
    routed,
    w_query,
    w_key,
    w_value,
    w_out,
    w_up,
    w_down,
    w_route,
    gain_attn,
    gain_mlp,
    cotangent,
):
    half_width = tokens.shape[3]
    capacity = routed.shape[2]
    offset = lax.axis_index("tensor") * half_width
    width = half_width * lax.axis_size("tensor")
    score_scale = HD ** (-0.5)
    causal = lax.broadcasted_iota(jnp.int32, (capacity, capacity), 0) >= lax.broadcasted_iota(
        jnp.int32, (capacity, capacity), 1
    )

    def sequence_step(gradients, weight_rows, weight_cols, tok_seq, chosen, cot_seq):
        full_query, full_key, full_value, full_up, full_route, full_gain1, full_gain2 = weight_rows
        full_out, full_down = weight_cols
        g_query, g_key, g_value, g_up, g_route, g_gain1, g_gain2, g_out, g_down = gradients
        route_f32 = full_route.astype(jnp.float32)
        gain1_f32 = full_gain1.astype(jnp.float32)
        gain2_f32 = full_gain2.astype(jnp.float32)
        rows_half = jnp.take(tok_seq, chosen, axis=0)
        cot_half = jnp.take(cot_seq, chosen, axis=0)
        routed_rows, cot_rows = (
            lax.all_gather(rows_half, "tensor", axis=1, tiled=True),
            lax.all_gather(cot_half, "tensor", axis=1, tiled=True),
        )
        rows_f32 = routed_rows.astype(jnp.float32)
        rows_half_f32 = rows_half.astype(jnp.float32)
        cot_half_f32 = cot_half.astype(jnp.float32)
        route_logit = dense(routed_rows, full_route)
        route_gate = jax.nn.sigmoid(route_logit)
        normed = rms_norm(rows_f32, gain1_f32).astype(jnp.bfloat16)
        queries = dense(normed, full_query).astype(jnp.bfloat16).reshape(capacity, -1, HD)
        key_rows = dense(normed, full_key).astype(jnp.bfloat16).reshape(capacity, -1, HD)
        value_rows = dense(normed, full_value).astype(jnp.bfloat16).reshape(capacity, -1, HD)
        scores = (
            jnp.einsum("qhd,khd->hqk", queries, key_rows, preferred_element_type=jnp.float32)
            * score_scale
        )
        scores = jnp.where(causal[None], scores, -1e30)
        log_total = jax.nn.logsumexp(scores, axis=-1, keepdims=True)
        probs_low = jnp.exp(scores - log_total).astype(jnp.bfloat16)
        mixed_heads = jnp.einsum(
            "hqk,khd->qhd", probs_low, value_rows, preferred_element_type=jnp.float32
        )
        mixed_heads = mixed_heads.astype(jnp.bfloat16).reshape(capacity, -1)
        attended = lax.psum(dense(mixed_heads, full_out).astype(jnp.bfloat16), "tensor").astype(
            jnp.float32
        )
        hidden = rows_f32 + attended
        normed2 = rms_norm(hidden, gain2_f32).astype(jnp.bfloat16)
        up_proj = dense(normed2, full_up)
        activated = jax.nn.gelu(up_proj).astype(jnp.bfloat16)
        down_out = lax.psum(dense(activated, full_down).astype(jnp.bfloat16), "tensor").astype(
            jnp.float32
        )
        branch = attended + down_out
        branch_half = lax.dynamic_slice_in_dim(branch, offset, half_width, 1)
        d_logit = (
            jnp.sum(cot_rows.astype(jnp.float32) * branch, -1) * route_gate * (1.0 - route_gate)
        )
        new_rows = (rows_half_f32 + route_gate[:, None] * branch_half).astype(jnp.bfloat16)
        out_seq = tok_seq.at[chosen].set(new_rows)
        cot_f32 = cot_rows.astype(jnp.float32)
        d_branch = route_gate[:, None] * cot_f32
        d_down = d_branch.astype(jnp.bfloat16)
        up_again = dense(lax.optimization_barrier(normed2), full_up)
        act_again = jax.nn.gelu(up_again).astype(jnp.bfloat16)
        g_down = g_down + dense(act_again.T, d_down)
        d_act = dense(d_down, full_down.T)
        gelu_value, gelu_back = jax.vjp(jax.nn.gelu, up_again)
        d_upper = gelu_back(d_act)[0].astype(jnp.bfloat16)
        g_up = g_up + dense(normed2.T, d_upper)
        d_normed2 = lax.psum(dense(d_upper, full_up.T).astype(jnp.bfloat16), "tensor").astype(
            jnp.float32
        )
        norm2_value, norm2_back = jax.vjp(rms_norm, hidden, gain2_f32)
        d_hidden, d_gain2 = norm2_back(d_normed2)
        g_gain2 = g_gain2 + d_gain2
        d_attended = (d_branch + d_hidden).astype(jnp.bfloat16)
        g_out = g_out + dense(mixed_heads.T, d_attended)
        d_mixed = dense(d_attended, full_out.T).astype(jnp.bfloat16).reshape(capacity, -1, HD)
        scores_again = (
            jnp.einsum("qhd,khd->hqk", queries, key_rows, preferred_element_type=jnp.float32)
            * score_scale
        )
        scores_again = jnp.where(causal[None], scores_again, -1e30)
        attn_probs = jnp.exp(scores_again - log_total)
        probs_again = attn_probs.astype(jnp.bfloat16)
        d_values = jnp.einsum(
            "hqk,qhd->khd", probs_again, d_mixed, preferred_element_type=jnp.float32
        )
        d_values = d_values.astype(jnp.bfloat16).reshape(capacity, -1)
        d_probs = jnp.einsum(
            "qhd,khd->hqk", d_mixed, value_rows, preferred_element_type=jnp.float32
        )
        d_scores = attn_probs * (d_probs - jnp.sum(d_probs * attn_probs, -1, keepdims=True))
        d_scores = d_scores.astype(jnp.bfloat16)
        d_queries = (
            jnp.einsum("hqk,khd->qhd", d_scores, key_rows, preferred_element_type=jnp.float32)
            * score_scale
        )
        d_queries = d_queries.astype(jnp.bfloat16).reshape(capacity, -1)
        d_keys = (
            jnp.einsum("hqk,qhd->khd", d_scores, queries, preferred_element_type=jnp.float32)
            * score_scale
        )
        d_keys = d_keys.astype(jnp.bfloat16).reshape(capacity, -1)
        g_query = g_query + dense(normed.T, d_queries)
        g_key = g_key + dense(normed.T, d_keys)
        g_value = g_value + dense(normed.T, d_values)
        partial_normed = (
            dense(d_queries, full_query.T)
            + dense(d_keys, full_key.T)
            + dense(d_values, full_value.T)
        )
        d_hidden_half = lax.dynamic_slice_in_dim(d_hidden, offset, half_width, 1)
        route_half = lax.dynamic_slice_in_dim(route_f32, offset, half_width, 0)
        d_normed = lax.psum(partial_normed.astype(jnp.bfloat16), "tensor").astype(jnp.float32)
        norm1_value, norm1_back = jax.vjp(rms_norm, rows_f32, gain1_f32)
        d_rows_norm, d_gain1 = norm1_back(d_normed)
        g_gain1 = g_gain1 + d_gain1
        d_norm_half = lax.dynamic_slice_in_dim(d_rows_norm, offset, half_width, 1)
        g_route = g_route + jnp.dot(
            rows_f32.T, d_logit, precision=lax.Precision.HIGHEST, preferred_element_type=jnp.float32
        )
        d_half = d_hidden_half + d_norm_half + d_logit[:, None] * route_half[None, :]
        grad_rows_new = (cot_half_f32 + d_half).astype(jnp.bfloat16)
        grad_seq = cot_seq.at[chosen].set(grad_rows_new)
        new_gradients = (g_query, g_key, g_value, g_up, g_route, g_gain1, g_gain2, g_out, g_down)
        return (new_gradients, out_seq, grad_seq)

    def micro_step(gradients, micro_inputs):
        tok_micro, routed_micro, cot_micro = micro_inputs
        weight_rows = (
            lax.all_gather(w_query, "dp", axis=0, tiled=True),
            lax.all_gather(w_key, "dp", axis=0, tiled=True),
            lax.all_gather(w_value, "dp", axis=0, tiled=True),
            lax.all_gather(w_up, "dp", axis=0, tiled=True),
            lax.all_gather(w_route, "dp", axis=0, tiled=True),
            lax.all_gather(gain_attn, "dp", axis=0, tiled=True),
            lax.all_gather(gain_mlp, "dp", axis=0, tiled=True),
        )
        weight_cols = (
            lax.all_gather(w_out, "dp", axis=1, tiled=True),
            lax.all_gather(w_down, "dp", axis=1, tiled=True),
        )

        def sequence_scan(carried, seq_inputs):
            tok_seq, chosen, cot_seq = seq_inputs
            updated, out_seq, grad_seq = sequence_step(
                carried, weight_rows, weight_cols, tok_seq, chosen, cot_seq
            )
            return (updated, (out_seq, grad_seq))

        gradients, seq_results = lax.scan(
            sequence_scan, gradients, (tok_micro, routed_micro, cot_micro)
        )
        return (gradients, seq_results)

    zero_grads = (
        jnp.zeros((width, w_query.shape[1]), jnp.float32),
        jnp.zeros((width, w_key.shape[1]), jnp.float32),
        jnp.zeros((width, w_value.shape[1]), jnp.float32),
        jnp.zeros((width, w_up.shape[1]), jnp.float32),
        jnp.zeros((width,), jnp.float32),
        jnp.zeros((width,), jnp.float32),
        jnp.zeros((width,), jnp.float32),
        jnp.zeros((w_out.shape[0], width), jnp.float32),
        jnp.zeros((w_down.shape[0], width), jnp.float32),
    )
    totals, results = lax.scan(micro_step, zero_grads, (tokens, routed, cotangent))
    output, input_grad = results
    g_query, g_key, g_value, g_up, g_route, g_gain1, g_gain2, g_out, g_down = totals
    grad_query, grad_key, grad_value, grad_up, grad_route, grad_gain_attn, grad_gain_mlp = (
        lax.psum_scatter(g_query, "dp", scatter_dimension=0, tiled=True),
        lax.psum_scatter(g_key, "dp", scatter_dimension=0, tiled=True),
        lax.psum_scatter(g_value, "dp", scatter_dimension=0, tiled=True),
        lax.psum_scatter(g_up, "dp", scatter_dimension=0, tiled=True),
        lax.psum_scatter(g_route, "dp", scatter_dimension=0, tiled=True),
        lax.psum_scatter(g_gain1, "dp", scatter_dimension=0, tiled=True),
        lax.psum_scatter(g_gain2, "dp", scatter_dimension=0, tiled=True),
    )
    grad_out, grad_down = (
        lax.psum_scatter(g_out, "dp", scatter_dimension=1, tiled=True),
        lax.psum_scatter(g_down, "dp", scatter_dimension=1, tiled=True),
    )
    return (
        output,
        input_grad,
        grad_query,
        grad_key,
        grad_value,
        grad_out,
        grad_up,
        grad_down,
        grad_route,
        grad_gain_attn,
        grad_gain_mlp,
    )


def solution(mesh):
    placed = (
        P(None, "dp", None, "tensor"),
        P(None, "dp", None),
        P("dp", "tensor"),
        P("dp", "tensor"),
        P("dp", "tensor"),
        P("tensor", "dp"),
        P("dp", "tensor"),
        P("tensor", "dp"),
        P("dp"),
        P("dp"),
        P("dp"),
        P(None, "dp", None, "tensor"),
    )
    return jax.shard_map(
        shards,
        mesh=mesh,
        in_specs=placed,
        out_specs=(
            P(None, "dp", None, "tensor"),
            P(None, "dp", None, "tensor"),
            P("dp", "tensor"),
            P("dp", "tensor"),
            P("dp", "tensor"),
            P("tensor", "dp"),
            P("dp", "tensor"),
            P("tensor", "dp"),
            P("dp"),
            P("dp"),
            P("dp"),
        ),
        check_vma=False,
    )
```

profile of v0, /device:TPU:10, one launch (start us, length us, event | category | flops | bytes accessed | tf_op | source)
XLA Modules:
  0.0 2646.1 jit_solution(17404735948335513344)
XLA Ops:
  8.1 1940.2 %while.33 = (s32[]{:T(128)}, f32[1024,512]{1,0:T(8,128)}, f32[1024,512]{1,0:T(8,128)}, f32[1024,512]{1,0:T(8,128)}, f32[1024,2048]{1,0:T(8,128)}, /*index=5*/f32...) while((s32[]{:T(128)}, f32[1024,512]{1,0:T(8,128)}, ...), condition=%wide.region_17.19_spmd.clone, body=%wide.region_0.18_spmd.clone.sunk | while | flops 11211988992 | bytes 388675808 | solution.py:199
  69.3 55.2 %all-gather.7.cloned.1.call-done = bf16[1024,512]{1,0:T(8,128)(2,1)} async-done(((bf16[64,512]{1,0:T(8,128)(2,1)}), bf16[1024,512]{1,0:T(8,128)(2,1)}) %all-gather.7.cloned.1.call-update) | async-done | bytes 1048592 | tf_op jit(solution)/shard_map/while/body/eval_jaxpr/all_gather | solution.py:164
  126.3 55.0 %all-gather.11.cloned.1.call-done = bf16[1024,512]{1,0:T(8,128)(2,1)} async-done(((bf16[64,512]{1,0:T(8,128)(2,1)}), bf16[1024,512]{1,0:T(8,128)(2,1)}) %all-gather.11.cloned.1.call-update) | async-done | bytes 1048592 | tf_op jit(solution)/shard_map/while/body/eval_jaxpr/all_gather | solution.py:165
  263.0 76.7 %all-gather.15.cloned.1.call-done = bf16[1024,2048]{1,0:T(8,128)(2,1)} async-done(((bf16[64,2048]{1,0:T(8,128)(2,1)}), bf16[1024,2048]{1,0:T(8,128)(2,1)}) %all-gather.15.cloned.1.call-update) | async-done | bytes 4194320 | tf_op jit(solution)/shard_map/while/body/eval_jaxpr/all_gather | solution.py:166
  344.5 73.0 %all-gather.17.cloned.1.call-done = bf16[2048,1024]{0,1:T(8,128)(2,1)} async-done(((bf16[2048,64]{0,1:T(8,128)(2,1)}), bf16[2048,1024]{0,1:T(8,128)(2,1)}) %all-gather.17.cloned.1.call-update) | async-done | bytes 4194320 | tf_op jit(solution)/shard_map/while/body/eval_jaxpr/all_gather | solution.py:173
  554.0 55.2 %all-gather.7.cloned.1.call-done = bf16[1024,512]{1,0:T(8,128)(2,1)} async-done(((bf16[64,512]{1,0:T(8,128)(2,1)}), bf16[1024,512]{1,0:T(8,128)(2,1)}) %all-gather.7.cloned.1.call-update) | async-done | bytes 1048592 | tf_op jit(solution)/shard_map/while/body/eval_jaxpr/all_gather | solution.py:164
  611.0 54.9 %all-gather.11.cloned.1.call-done = bf16[1024,512]{1,0:T(8,128)(2,1)} async-done(((bf16[64,512]{1,0:T(8,128)(2,1)}), bf16[1024,512]{1,0:T(8,128)(2,1)}) %all-gather.11.cloned.1.call-update) | async-done | bytes 1048592 | tf_op jit(solution)/shard_map/while/body/eval_jaxpr/all_gather | solution.py:165
  747.7 76.7 %all-gather.15.cloned.1.call-done = bf16[1024,2048]{1,0:T(8,128)(2,1)} async-done(((bf16[64,2048]{1,0:T(8,128)(2,1)}), bf16[1024,2048]{1,0:T(8,128)(2,1)}) %all-gather.15.cloned.1.call-update) | async-done | bytes 4194320 | tf_op jit(solution)/shard_map/while/body/eval_jaxpr/all_gather | solution.py:166
  829.2 72.8 %all-gather.17.cloned.1.call-done = bf16[2048,1024]{0,1:T(8,128)(2,1)} async-done(((bf16[2048,64]{0,1:T(8,128)(2,1)}), bf16[2048,1024]{0,1:T(8,128)(2,1)}) %all-gather.17.cloned.1.call-update) | async-done | bytes 4194320 | tf_op jit(solution)/shard_map/while/body/eval_jaxpr/all_gather | solution.py:173
  1038.9 55.0 %all-gather.7.cloned.1.call-done = bf16[1024,512]{1,0:T(8,128)(2,1)} async-done(((bf16[64,512]{1,0:T(8,128)(2,1)}), bf16[1024,512]{1,0:T(8,128)(2,1)}) %all-gather.7.cloned.1.call-update) | async-done | bytes 1048592 | tf_op jit(solution)/shard_map/while/body/eval_jaxpr/all_gather | solution.py:164
  1095.7 55.0 %all-gather.11.cloned.1.call-done = bf16[1024,512]{1,0:T(8,128)(2,1)} async-done(((bf16[64,512]{1,0:T(8,128)(2,1)}), bf16[1024,512]{1,0:T(8,128)(2,1)}) %all-gather.11.cloned.1.call-update) | async-done | bytes 1048592 | tf_op jit(solution)/shard_map/while/body/eval_jaxpr/all_gather | solution.py:165
  1232.7 76.7 %all-gather.15.cloned.1.call-done = bf16[1024,2048]{1,0:T(8,128)(2,1)} async-done(((bf16[64,2048]{1,0:T(8,128)(2,1)}), bf16[1024,2048]{1,0:T(8,128)(2,1)}) %all-gather.15.cloned.1.call-update) | async-done | bytes 4194320 | tf_op jit(solution)/shard_map/while/body/eval_jaxpr/all_gather | solution.py:166
  1314.2 73.0 %all-gather.17.cloned.1.call-done = bf16[2048,1024]{0,1:T(8,128)(2,1)} async-done(((bf16[2048,64]{0,1:T(8,128)(2,1)}), bf16[2048,1024]{0,1:T(8,128)(2,1)}) %all-gather.17.cloned.1.call-update) | async-done | bytes 4194320 | tf_op jit(solution)/shard_map/while/body/eval_jaxpr/all_gather | solution.py:173
  1524.0 55.2 %all-gather.7.cloned.1.call-done = bf16[1024,512]{1,0:T(8,128)(2,1)} async-done(((bf16[64,512]{1,0:T(8,128)(2,1)}), bf16[1024,512]{1,0:T(8,128)(2,1)}) %all-gather.7.cloned.1.call-update) | async-done | bytes 1048592 | tf_op jit(solution)/shard_map/while/body/eval_jaxpr/all_gather | solution.py:164
  1581.0 54.9 %all-gather.11.cloned.1.call-done = bf16[1024,512]{1,0:T(8,128)(2,1)} async-done(((bf16[64,512]{1,0:T(8,128)(2,1)}), bf16[1024,512]{1,0:T(8,128)(2,1)}) %all-gather.11.cloned.1.call-update) | async-done | bytes 1048592 | tf_op jit(solution)/shard_map/while/body/eval_jaxpr/all_gather | solution.py:165
  1639.1 53.7 %all-gather.13.cloned.1.call-done = bf16[512,1024]{0,1:T(8,128)(2,1)} async-done(((bf16[512,64]{0,1:T(8,128)(2,1)}), bf16[512,1024]{0,1:T(8,128)(2,1)}) %all-gather.13.cloned.1.call-update) | async-done | bytes 1048592 | tf_op jit(solution)/shard_map/while/body/eval_jaxpr/all_gather | solution.py:172
  1717.9 76.7 %all-gather.15.cloned.1.call-done = bf16[1024,2048]{1,0:T(8,128)(2,1)} async-done(((bf16[64,2048]{1,0:T(8,128)(2,1)}), bf16[1024,2048]{1,0:T(8,128)(2,1)}) %all-gather.15.cloned.1.call-update) | async-done | bytes 4194320 | tf_op jit(solution)/shard_map/while/body/eval_jaxpr/all_gather | solution.py:166
  1799.4 73.0 %all-gather.17.cloned.1.call-done = bf16[2048,1024]{0,1:T(8,128)(2,1)} async-done(((bf16[2048,64]{0,1:T(8,128)(2,1)}), bf16[2048,1024]{0,1:T(8,128)(2,1)}) %all-gather.17.cloned.1.call-update) | async-done | bytes 4194320 | tf_op jit(solution)/shard_map/while/body/eval_jaxpr/all_gather | solution.py:173
  1964.4 65.4 %all-reduce.11 = (f32[1024]{0:T(1024)S(1)}, f32[1024]{0:T(1024)S(1)}, f32[1024]{0:T(1024)S(1)}) all-reduce(f32[1024]{0:T(1024)S(1)} %get-tuple-element.429, f32[1024]{0:T(1024)S(1)} %get-tuple-element.430, f32[1024]{0:T(1024)S(1)} %get-tuple-element.431), channel_id=8, replica_groups=mesh['dp'=16,'tensor'=2] {'dp'}, use_global_device_ids=true, to_apply=%region_24.26.clone | all-reduce | flops 3072 | bytes 24576
  2031.5 72.3 %reduce-scatter.11.cloned.1.call-done = f32[64,512]{1,0:T(8,128)} async-done(((f32[1024,512]{1,0:T(8,128)}), f32[64,512]{1,0:T(8,128)}) %reduce-scatter.11.cloned.1.call-update) | async-done | bytes 131088 | tf_op jit(solution)/shard_map/reduce_scatter | solution.py:205
  2103.9 80.7 %reduce-scatter.7.cloned.1.call-done = f32[64,512]{1,0:T(8,128)} async-done(((f32[1024,512]{1,0:T(8,128)}), f32[64,512]{1,0:T(8,128)}) %reduce-scatter.7.cloned.1.call-update) | async-done | bytes 131088 | tf_op jit(solution)/shard_map/reduce_scatter | solution.py:203
  2184.6 80.9 %reduce-scatter.9.cloned.1.call-done = f32[64,512]{1,0:T(8,128)} async-done(((f32[1024,512]{1,0:T(8,128)}), f32[64,512]{1,0:T(8,128)}) %reduce-scatter.9.cloned.1.call-update) | async-done | bytes 131088 | tf_op jit(solution)/shard_map/reduce_scatter | solution.py:204
  2265.5 190.3 %reduce-scatter.17.cloned.1.call-done = f32[2048,64]{0,1:T(8,128)} async-done(((f32[2048,1024]{0,1:T(8,128)}), f32[2048,64]{0,1:T(8,128)}) %reduce-scatter.17.cloned.1.call-update) | async-done | bytes 524304 | tf_op jit(solution)/shard_map/reduce_scatter | solution.py:213
  2455.9 183.1 %reduce-scatter.15.cloned.1.call-done = f32[64,2048]{1,0:T(8,128)} async-done(((f32[1024,2048]{1,0:T(8,128)}), f32[64,2048]{1,0:T(8,128)}) %reduce-scatter.15.cloned.1.call-update) | async-done | bytes 524304 | tf_op jit(solution)/shard_map/reduce_scatter | solution.py:206
  (759 shorter events, 859.2 us)
Async XLA Ops:
  9.6 171.7 %all-gather.11.cloned.1.call-start = ((), (), s32[]{:S(2)}) async-start(), calls=%async_computation.14 | async-start | bytes 1114112 | tf_op jit(solution)/shard_map/while/body/eval_jaxpr/all_gather | solution.py:165
  10.4 227.7 %all-gather.13.cloned.1.call-start = ((), (), s32[]{:S(2)}) async-start(), calls=%async_computation.15 | async-start | bytes 1114112 | tf_op jit(solution)/shard_map/while/body/eval_jaxpr/all_gather | solution.py:172
  10.9 248.7 %all-reduce.20.cloned.1.call-start = ((), (), s32[]{:S(2)}) async-start(), calls=%async_computation.16 | async-start | bytes 1048576 | tf_op jit(solution)/shard_map/while/body/eval_jaxpr/while/body/eval_jaxpr/psum | solution.py:74
  241.2 176.3 %all-gather.17.cloned.1.call-start = ((), (), s32[]{:S(2)}) async-start(), calls=%async_computation.18 | async-start | bytes 4456448 | tf_op jit(solution)/shard_map/while/body/eval_jaxpr/all_gather | solution.py:173
  241.9 209.8 %all-reduce.22.cloned.1.call-start = ((), (), s32[]{:S(2)}) async-start(), calls=%async_computation.19 | async-start | bytes 2097152 | tf_op jit(solution)/shard_map/while/body/eval_jaxpr/while/body/eval_jaxpr/psum | solution.py:101
  494.7 171.2 %all-gather.11.cloned.1.call-start = ((), (), s32[]{:S(2)}) async-start(), calls=%async_computation.14 | async-start | bytes 1114112 | tf_op jit(solution)/shard_map/while/body/eval_jaxpr/all_gather | solution.py:165
  495.3 227.5 %all-gather.13.cloned.1.call-start = ((), (), s32[]{:S(2)}) async-start(), calls=%async_computation.15 | async-start | bytes 1114112 | tf_op jit(solution)/shard_map/while/body/eval_jaxpr/all_gather | solution.py:172
  496.1 248.3 %all-reduce.20.cloned.1.call-start = ((), (), s32[]{:S(2)}) async-start(), calls=%async_computation.16 | async-start | bytes 1048576 | tf_op jit(solution)/shard_map/while/body/eval_jaxpr/while/body/eval_jaxpr/psum | solution.py:74
  725.9 176.2 %all-gather.17.cloned.1.call-start = ((), (), s32[]{:S(2)}) async-start(), calls=%async_computation.18 | async-start | bytes 4456448 | tf_op jit(solution)/shard_map/while/body/eval_jaxpr/all_gather | solution.py:173
  726.5 209.8 %all-reduce.22.cloned.1.call-start = ((), (), s32[]{:S(2)}) async-start(), calls=%async_computation.19 | async-start | bytes 2097152 | tf_op jit(solution)/shard_map/while/body/eval_jaxpr/while/body/eval_jaxpr/psum | solution.py:101
  979.3 171.5 %all-gather.11.cloned.1.call-start = ((), (), s32[]{:S(2)}) async-start(), calls=%async_computation.14 | async-start | bytes 1114112 | tf_op jit(solution)/shard_map/while/body/eval_jaxpr/all_gather | solution.py:165
  980.0 227.6 %all-gather.13.cloned.1.call-start = ((), (), s32[]{:S(2)}) async-start(), calls=%async_computation.15 | async-start | bytes 1114112 | tf_op jit(solution)/shard_map/while/body/eval_jaxpr/all_gather | solution.py:172
  980.8 248.6 %all-reduce.20.cloned.1.call-start = ((), (), s32[]{:S(2)}) async-start(), calls=%async_computation.16 | async-start | bytes 1048576 | tf_op jit(solution)/shard_map/while/body/eval_jaxpr/while/body/eval_jaxpr/psum | solution.py:74
  1210.7 176.5 %all-gather.17.cloned.1.call-start = ((), (), s32[]{:S(2)}) async-start(), calls=%async_computation.18 | async-start | bytes 4456448 | tf_op jit(solution)/shard_map/while/body/eval_jaxpr/all_gather | solution.py:173
  1211.5 209.9 %all-reduce.22.cloned.1.call-start = ((), (), s32[]{:S(2)}) async-start(), calls=%async_computation.19 | async-start | bytes 2097152 | tf_op jit(solution)/shard_map/while/body/eval_jaxpr/while/body/eval_jaxpr/psum | solution.py:101
  1464.6 171.3 %all-gather.11.cloned.1.call-start = ((), (), s32[]{:S(2)}) async-start(), calls=%async_computation.14 | async-start | bytes 1114112 | tf_op jit(solution)/shard_map/while/body/eval_jaxpr/all_gather | solution.py:165
  1465.2 227.6 %all-gather.13.cloned.1.call-start = ((), (), s32[]{:S(2)}) async-start(), calls=%async_computation.15 | async-start | bytes 1114112 | tf_op jit(solution)/shard_map/while/body/eval_jaxpr/all_gather | solution.py:172
  1465.9 248.6 %all-reduce.20.cloned.1.call-start = ((), (), s32[]{:S(2)}) async-start(), calls=%async_computation.16 | async-start | bytes 1048576 | tf_op jit(solution)/shard_map/while/body/eval_jaxpr/while/body/eval_jaxpr/psum | solution.py:74
  1695.9 176.5 %all-gather.17.cloned.1.call-start = ((), (), s32[]{:S(2)}) async-start(), calls=%async_computation.18 | async-start | bytes 4456448 | tf_op jit(solution)/shard_map/while/body/eval_jaxpr/all_gather | solution.py:173
  1696.6 209.9 %all-reduce.22.cloned.1.call-start = ((), (), s32[]{:S(2)}) async-start(), calls=%async_computation.19 | async-start | bytes 2097152 | tf_op jit(solution)/shard_map/while/body/eval_jaxpr/while/body/eval_jaxpr/psum | solution.py:101
  1951.8 232.8 %reduce-scatter.7.cloned.1.call-start = ((), (), s32[]{:S(2)}) async-start(), calls=%async_computation.6 | async-start | bytes 2228224 | tf_op jit(solution)/shard_map/reduce_scatter | solution.py:203
  1952.4 313.1 %reduce-scatter.9.cloned.1.call-start = ((), (), s32[]{:S(2)}) async-start(), calls=%async_computation.7 | async-start | bytes 2228224 | tf_op jit(solution)/shard_map/reduce_scatter | solution.py:204
  1953.1 502.7 %reduce-scatter.17.cloned.1.call-start = ((), (), s32[]{:S(2)}) async-start(), calls=%async_computation.11 | async-start | bytes 8912896 | tf_op jit(solution)/shard_map/reduce_scatter | solution.py:213
  1962.4 676.5 %reduce-scatter.15.cloned.1.call-start = ((), (), s32[]{:S(2)}) async-start(), calls=%async_computation.10 | async-start | bytes 8912896 | tf_op jit(solution)/shard_map/reduce_scatter | solution.py:206
  (183 other events, 2725.6 us)
Sparse Core Ops, SparseCore 0:
  11.7 55.6 all-gather.8
  70.2 54.2 all-gather.6
  127.2 54.0 all-gather.10
  184.0 54.0 all-gather.12
  262.6 76.9 all-gather.14
  342.8 74.6 all-gather.16
  496.7 55.4 all-gather.8
  554.9 54.2 all-gather.6
  611.8 54.0 all-gather.10
  668.7 54.0 all-gather.12
  747.3 76.9 all-gather.14
  827.3 74.6 all-gather.16
  981.6 55.4 all-gather.8
  1039.6 54.2 all-gather.6
  1096.6 54.0 all-gather.10
  1153.5 54.0 all-gather.12
  1232.3 76.9 all-gather.14
  1312.5 74.6 all-gather.16
  1466.7 55.4 all-gather.8
  1524.9 54.2 all-gather.6
  1581.8 54.0 all-gather.10
  1638.7 54.0 all-gather.12
  1717.5 76.9 all-gather.14
  1797.7 74.6 all-gather.16
  (12 shorter events, 228.2 us)
Sparse Core Ops, SparseCore 1:
  1951.6 72.0 reduce-scatter.12
  2026.4 77.5 reduce-scatter.10
  2106.6 77.9 reduce-scatter.6
  2187.5 78.0 reduce-scatter.8
  2268.4 187.4 reduce-scatter.16
  2458.7 180.1 reduce-scatter.14
where the time goes:
time: 2650 us
  waiting for transfers between devices  2020 us (76%)
  matrix products  212 us (8%)
  blocking collectives  209 us (8%)
  local copies, waits for them, and re-layouts  103 us (4%)
  other arithmetic  83.7 us (3%)
    all_gather x4, waiting for transfers between devices, micro_step(): lax.all_gather(w_up, 'dp', axis=0, tiled=True)  307 us
    all_gather x4, waiting for transfers between devices, micro_step(): lax.all_gather(w_down, 'dp', axis=1, tiled=True)  292 us
    all_gather x4, waiting for transfers between devices, micro_step(): lax.all_gather(w_key, 'dp', axis=0, tiled=True)  221 us
    all_gather x4, waiting for transfers between devices, micro_step(): lax.all_gather(w_value, 'dp', axis=0, tiled=True)  220 us
    all_gather x4, waiting for transfers between devices, micro_step(): lax.all_gather(w_out, 'dp', axis=1, tiled=True)  215 us
    dot_general x76, matrix products, dense(): return jnp.dot(left, right, preferred_element_type=jnp.float32)  200 us
    reduce_scatter x1, waiting for transfers between devices, shards(): lax.psum_scatter(g_down, 'dp', scatter_dimension=1, tiled=True)  190 us
    reduce_scatter x1, waiting for transfers between devices, shards(): lax.psum_scatter(g_up, 'dp', scatter_dimension=0, tiled=True)  183 us
  transfers between devices with their start and end apart: 42, of which 41 were waited for; matrix products, arithmetic and copies ran while one was open for 8% of the time, Pallas kernels for 0%

commit v1 on v0

--- a/solution.py
+++ b/solution.py
@@ -1,3 +1,4 @@
+import functools
 import jax
 import jax.numpy as jnp
 from jax import lax
@@ -5,6 +6,34 @@
 
 HD = 64
 eps_norm = 1e-05
+
+
+def _work_blocks(block_in, join_dim):
+    carry_in = list(block_in.shape[1:])
+    carry_in[join_dim] *= block_in.shape[0]
+    v_next = jnp.moveaxis(block_in, 0, join_dim).reshape(carry_in)
+    return v_next
+
+
+def produce_bands(u_in, device_axis):
+    new = u_in[None]
+    n_chips = lax.axis_size(device_axis)
+    for hop_no in range(n_chips.bit_length() - 1):
+        spare = 1 << hop_no
+        small = tuple(((tick, tick ^ spare) for tick in range(n_chips)))
+        o_now = lax.ppermute(new, device_axis, small)
+        y2 = jnp.stack([new, o_now])
+        b_next = lax.axis_index(device_axis) >> hop_no & 1
+        new = jnp.where(b_next == 0, y2, y2[::-1]).reshape(-1, *u_in.shape)
+    return new
+
+
+def _proceed_strips_all(incoming_x, u, array_axis):
+    opened = _work_blocks(produce_bands(incoming_x, u), array_axis)
+    return opened
+
+
+lead_table_up = functools.partial(_proceed_strips_all, u="dp", array_axis=0)
 
 
 def rms_norm(values, gain):
@@ -161,7 +190,7 @@
         tok_micro, routed_micro, cot_micro = micro_inputs
         weight_rows = (
             lax.all_gather(w_query, "dp", axis=0, tiled=True),
-            lax.all_gather(w_key, "dp", axis=0, tiled=True),
+            lead_table_up(w_key),
             lax.all_gather(w_value, "dp", axis=0, tiled=True),
             lax.all_gather(w_up, "dp", axis=0, tiled=True),
             lax.all_gather(w_route, "dp", axis=0, tiled=True),

time: 2650 us -> 2500 us (0.943)
  waiting for transfers between devices: 2020 us -> 1780 us
  blocking collectives: 209 us -> 265 us
    all_gather x4 -> x0, waiting for transfers between devices: 221 us -> none  [micro_step(): lax.all_gather(w_key, 'dp', axis=0, tiled=True)]
    reduce_scatter x1, waiting for transfers between devices: 80.7 us -> 0.01 us  [shards(): lax.psum_scatter(g_query, 'dp', scatter_dimension=0, tiled=True)]
    reduce_scatter x1, waiting for transfers between devices: 0.01 us -> 80 us  [shards(): lax.psum_scatter(g_out, 'dp', scatter_dimension=1, tiled=True)]
    while x4, blocking collectives: 126 us -> 181 us
    all_gather x4, waiting for transfers between devices: 39.9 us -> 2.42 us  [micro_step(): lax.all_gather(w_query, 'dp', axis=0, tiled=True)]
  transfers between devices with their start and end apart: 42 -> 51, of which waited for: 41 -> 39; matrix products, arithmetic and copies ran while one was open for 8% -> 9% of each run, Pallas kernels for 0% -> 0%
where the time goes in v1:
time: 2500 us; the launch traced here: 2490 us
  waiting for transfers between devices  1780 us (71%)
  blocking collectives  265 us (11%)
  matrix products  225 us (9%)
  local copies, waits for them, and re-layouts  97.1 us (4%)
  other arithmetic  87.4 us (3%)
    all_gather x4, waiting for transfers between devices, micro_step(): lax.all_gather(w_up, 'dp', axis=0, tiled=True)  307 us
    all_gather x4, waiting for transfers between devices, micro_step(): lax.all_gather(w_down, 'dp', axis=1, tiled=True)  291 us
    all_gather x4, waiting for transfers between devices, micro_step(): lax.all_gather(w_out, 'dp', axis=1, tiled=True)  215 us
    all_gather x4, waiting for transfers between devices, micro_step(): lax.all_gather(w_value, 'dp', axis=0, tiled=True)  214 us
    dot_general x76, matrix products, dense(): return jnp.dot(left, right, preferred_element_type=jnp.float32)  213 us
    reduce_scatter x1, waiting for transfers between devices, shards(): lax.psum_scatter(g_up, 'dp', scatter_dimension=0, tiled=True)  191 us
    reduce_scatter x1, waiting for transfers between devices, shards(): lax.psum_scatter(g_down, 'dp', scatter_dimension=1, tiled=True)  183 us
    while x4, blocking collectives  181 us
  transfers between devices with their start and end apart: 51, of which 39 were waited for; matrix products, arithmetic and copies ran while one was open for 9% of the time, Pallas kernels for 0%

profile of v1, /device:TPU:10, one launch (start us, length us, event | category | flops | bytes accessed | tf_op | source)
XLA Modules:
  0.0 2494.2 jit_solution(11550777376927756982)
XLA Ops:
  13.4 1783.8 %while.33 = (s32[]{:T(128)}, f32[1024,512]{1,0:T(8,128)}, f32[1024,512]{1,0:T(8,128)}, f32[1024,512]{1,0:T(8,128)}, f32[1024,2048]{1,0:T(8,128)}, /*index=5*/f32...) while((s32[]{:T(128)}, f32[1024,512]{1,0:T(8,128)}, ...), condition=%wide.region_17.19_spmd.clone, body=%wide.region_0.18_spmd.clone.sunk | while | flops 11213889536 | bytes 361085152 | solution.py:228
  85.5 55.0 %all-gather.8.cloned.1.call-done = bf16[1024,512]{1,0:T(8,128)(2,1)} async-done(((bf16[64,512]{1,0:T(8,128)(2,1)}), bf16[1024,512]{1,0:T(8,128)(2,1)}) %all-gather.8.cloned.1.call-update) | async-done | bytes 1048592 | tf_op jit(solution)/shard_map/while/body/eval_jaxpr/all_gather | solution.py:194
  143.7 53.7 %all-gather.10.cloned.1.call-done = bf16[512,1024]{0,1:T(8,128)(2,1)} async-done(((bf16[512,64]{0,1:T(8,128)(2,1)}), bf16[512,1024]{0,1:T(8,128)(2,1)}) %all-gather.10.cloned.1.call-update) | async-done | bytes 1048592 | tf_op jit(solution)/shard_map/while/body/eval_jaxpr/all_gather | solution.py:201
  222.3 76.7 %all-gather.12.cloned.1.call-done = bf16[1024,2048]{1,0:T(8,128)(2,1)} async-done(((bf16[64,2048]{1,0:T(8,128)(2,1)}), bf16[1024,2048]{1,0:T(8,128)(2,1)}) %all-gather.12.cloned.1.call-update) | async-done | bytes 4194320 | tf_op jit(solution)/shard_map/while/body/eval_jaxpr/all_gather | solution.py:195
  303.9 72.8 %all-gather.14.cloned.1.call-done = bf16[2048,1024]{0,1:T(8,128)(2,1)} async-done(((bf16[2048,64]{0,1:T(8,128)(2,1)}), bf16[2048,1024]{0,1:T(8,128)(2,1)}) %all-gather.14.cloned.1.call-update) | async-done | bytes 4194320 | tf_op jit(solution)/shard_map/while/body/eval_jaxpr/all_gather | solution.py:202
  531.9 52.9 %all-gather.8.cloned.1.call-done = bf16[1024,512]{1,0:T(8,128)(2,1)} async-done(((bf16[64,512]{1,0:T(8,128)(2,1)}), bf16[1024,512]{1,0:T(8,128)(2,1)}) %all-gather.8.cloned.1.call-update) | async-done | bytes 1048592 | tf_op jit(solution)/shard_map/while/body/eval_jaxpr/all_gather | solution.py:194
  588.0 53.7 %all-gather.10.cloned.1.call-done = bf16[512,1024]{0,1:T(8,128)(2,1)} async-done(((bf16[512,64]{0,1:T(8,128)(2,1)}), bf16[512,1024]{0,1:T(8,128)(2,1)}) %all-gather.10.cloned.1.call-update) | async-done | bytes 1048592 | tf_op jit(solution)/shard_map/while/body/eval_jaxpr/all_gather | solution.py:201
  666.6 76.8 %all-gather.12.cloned.1.call-done = bf16[1024,2048]{1,0:T(8,128)(2,1)} async-done(((bf16[64,2048]{1,0:T(8,128)(2,1)}), bf16[1024,2048]{1,0:T(8,128)(2,1)}) %all-gather.12.cloned.1.call-update) | async-done | bytes 4194320 | tf_op jit(solution)/shard_map/while/body/eval_jaxpr/all_gather | solution.py:195
  748.3 72.8 %all-gather.14.cloned.1.call-done = bf16[2048,1024]{0,1:T(8,128)(2,1)} async-done(((bf16[2048,64]{0,1:T(8,128)(2,1)}), bf16[2048,1024]{0,1:T(8,128)(2,1)}) %all-gather.14.cloned.1.call-update) | async-done | bytes 4194320 | tf_op jit(solution)/shard_map/while/body/eval_jaxpr/all_gather | solution.py:202
  925.9 45.8 %all-reduce.14 = (bf16[1024]{0:T(1024)(128)(2,1)S(1)}, bf16[1024]{0:T(1024)(128)(2,1)S(1)}, bf16[1024]{0:T(1024)(128)(2,1)S(1)}) all-reduce(bf16[1024]{0:T(1024)(128)(2,1)S(1)} %dynamic-update-slice.9, bf16[1024]{0:T(1024)(128)(2,1)S(1)} %dynamic-update-slice.10, ...), channel_id=1, replica_groups=mesh['dp'=16,'tensor'=2] {'dp'}, use_global_device_ids=true, to_apply=%add.1 | all-reduce | flops 3072 | bytes 12288 | tf_op jit(solution)/shard_map/while
  978.0 52.9 %all-gather.8.cloned.1.call-done = bf16[1024,512]{1,0:T(8,128)(2,1)} async-done(((bf16[64,512]{1,0:T(8,128)(2,1)}), bf16[1024,512]{1,0:T(8,128)(2,1)}) %all-gather.8.cloned.1.call-update) | async-done | bytes 1048592 | tf_op jit(solution)/shard_map/while/body/eval_jaxpr/all_gather | solution.py:194
  1034.1 53.7 %all-gather.10.cloned.1.call-done = bf16[512,1024]{0,1:T(8,128)(2,1)} async-done(((bf16[512,64]{0,1:T(8,128)(2,1)}), bf16[512,1024]{0,1:T(8,128)(2,1)}) %all-gather.10.cloned.1.call-update) | async-done | bytes 1048592 | tf_op jit(solution)/shard_map/while/body/eval_jaxpr/all_gather | solution.py:201
  1112.7 76.8 %all-gather.12.cloned.1.call-done = bf16[1024,2048]{1,0:T(8,128)(2,1)} async-done(((bf16[64,2048]{1,0:T(8,128)(2,1)}), bf16[1024,2048]{1,0:T(8,128)(2,1)}) %all-gather.12.cloned.1.call-update) | async-done | bytes 4194320 | tf_op jit(solution)/shard_map/while/body/eval_jaxpr/all_gather | solution.py:195
  1194.4 73.0 %all-gather.14.cloned.1.call-done = bf16[2048,1024]{0,1:T(8,128)(2,1)} async-done(((bf16[2048,64]{0,1:T(8,128)(2,1)}), bf16[2048,1024]{0,1:T(8,128)(2,1)}) %all-gather.14.cloned.1.call-update) | async-done | bytes 4194320 | tf_op jit(solution)/shard_map/while/body/eval_jaxpr/all_gather | solution.py:202
  1424.2 52.9 %all-gather.8.cloned.1.call-done = bf16[1024,512]{1,0:T(8,128)(2,1)} async-done(((bf16[64,512]{1,0:T(8,128)(2,1)}), bf16[1024,512]{1,0:T(8,128)(2,1)}) %all-gather.8.cloned.1.call-update) | async-done | bytes 1048592 | tf_op jit(solution)/shard_map/while/body/eval_jaxpr/all_gather | solution.py:194
  1480.3 53.5 %all-gather.10.cloned.1.call-done = bf16[512,1024]{0,1:T(8,128)(2,1)} async-done(((bf16[512,64]{0,1:T(8,128)(2,1)}), bf16[512,1024]{0,1:T(8,128)(2,1)}) %all-gather.10.cloned.1.call-update) | async-done | bytes 1048592 | tf_op jit(solution)/shard_map/while/body/eval_jaxpr/all_gather | solution.py:201
  1558.9 76.8 %all-gather.12.cloned.1.call-done = bf16[1024,2048]{1,0:T(8,128)(2,1)} async-done(((bf16[64,2048]{1,0:T(8,128)(2,1)}), bf16[1024,2048]{1,0:T(8,128)(2,1)}) %all-gather.12.cloned.1.call-update) | async-done | bytes 4194320 | tf_op jit(solution)/shard_map/while/body/eval_jaxpr/all_gather | solution.py:195
  1640.6 72.8 %all-gather.14.cloned.1.call-done = bf16[2048,1024]{0,1:T(8,128)(2,1)} async-done(((bf16[2048,64]{0,1:T(8,128)(2,1)}), bf16[2048,1024]{0,1:T(8,128)(2,1)}) %all-gather.14.cloned.1.call-update) | async-done | bytes 4194320 | tf_op jit(solution)/shard_map/while/body/eval_jaxpr/all_gather | solution.py:202
  1813.2 65.5 %all-reduce.11 = (f32[1024]{0:T(1024)S(1)}, f32[1024]{0:T(1024)S(1)}, f32[1024]{0:T(1024)S(1)}) all-reduce(f32[1024]{0:T(1024)S(1)} %get-tuple-element.432, f32[1024]{0:T(1024)S(1)} %get-tuple-element.433, f32[1024]{0:T(1024)S(1)} %get-tuple-element.434), channel_id=8, replica_groups=mesh['dp'=16,'tensor'=2] {'dp'}, use_global_device_ids=true, to_apply=%region_24.26.clone | all-reduce | flops 3072 | bytes 24576
  1880.5 72.0 %reduce-scatter.9.cloned.1.call-done = f32[64,512]{1,0:T(8,128)} async-done(((f32[1024,512]{1,0:T(8,128)}), f32[64,512]{1,0:T(8,128)}) %reduce-scatter.9.cloned.1.call-update) | async-done | bytes 131088 | tf_op jit(solution)/shard_map/reduce_scatter | solution.py:233
  1952.5 80.9 %reduce-scatter.11.cloned.1.call-done = f32[64,512]{1,0:T(8,128)} async-done(((f32[1024,512]{1,0:T(8,128)}), f32[64,512]{1,0:T(8,128)}) %reduce-scatter.11.cloned.1.call-update) | async-done | bytes 131088 | tf_op jit(solution)/shard_map/reduce_scatter | solution.py:234
  2033.3 80.0 %reduce-scatter.13.cloned.1.call-done = f32[512,64]{0,1:T(8,128)} async-done(((f32[512,1024]{0,1:T(8,128)}), f32[512,64]{0,1:T(8,128)}) %reduce-scatter.13.cloned.1.call-update) | async-done | bytes 131088 | tf_op jit(solution)/shard_map/reduce_scatter | solution.py:241
  2113.4 190.6 %reduce-scatter.15.cloned.1.call-done = f32[64,2048]{1,0:T(8,128)} async-done(((f32[1024,2048]{1,0:T(8,128)}), f32[64,2048]{1,0:T(8,128)}) %reduce-scatter.15.cloned.1.call-update) | async-done | bytes 524304 | tf_op jit(solution)/shard_map/reduce_scatter | solution.py:235
  2304.0 183.1 %reduce-scatter.17.cloned.1.call-done = f32[2048,64]{0,1:T(8,128)} async-done(((f32[2048,1024]{0,1:T(8,128)}), f32[2048,64]{0,1:T(8,128)}) %reduce-scatter.17.cloned.1.call-update) | async-done | bytes 524304 | tf_op jit(solution)/shard_map/reduce_scatter | solution.py:242
  (740 shorter events, 728.1 us)
Async XLA Ops:
  14.2 126.3 %all-gather.8.cloned.1.call-start = ((), (), s32[]{:S(2)}) async-start(), calls=%async_computation.13 | async-start | bytes 1114112 | tf_op jit(solution)/shard_map/while/body/eval_jaxpr/all_gather | solution.py:194
  14.9 182.5 %all-gather.10.cloned.1.call-start = ((), (), s32[]{:S(2)}) async-start(), calls=%async_computation.14 | async-start | bytes 1114112 | tf_op jit(solution)/shard_map/while/body/eval_jaxpr/all_gather | solution.py:201
  16.6 202.3 %all-reduce.20.cloned.1.call-start = ((), (), s32[]{:S(2)}) async-start(), calls=%async_computation.15 | async-start | bytes 1048576 | tf_op jit(solution)/shard_map/while/body/eval_jaxpr/while/body/eval_jaxpr/psum | solution.py:103
  200.5 176.2 %all-gather.14.cloned.1.call-start = ((), (), s32[]{:S(2)}) async-start(), calls=%async_computation.17 | async-start | bytes 4456448 | tf_op jit(solution)/shard_map/while/body/eval_jaxpr/all_gather | solution.py:202
  201.1 209.7 %all-reduce.22.cloned.1.call-start = ((), (), s32[]{:S(2)}) async-start(), calls=%async_computation.18 | async-start | bytes 2097152 | tf_op jit(solution)/shard_map/while/body/eval_jaxpr/while/body/eval_jaxpr/psum | solution.py:130
  459.5 125.3 %all-gather.8.cloned.1.call-start = ((), (), s32[]{:S(2)}) async-start(), calls=%async_computation.13 | async-start | bytes 1114112 | tf_op jit(solution)/shard_map/while/body/eval_jaxpr/all_gather | solution.py:194
  460.1 181.6 %all-gather.10.cloned.1.call-start = ((), (), s32[]{:S(2)}) async-start(), calls=%async_computation.14 | async-start | bytes 1114112 | tf_op jit(solution)/shard_map/while/body/eval_jaxpr/all_gather | solution.py:201
  461.8 201.5 %all-reduce.20.cloned.1.call-start = ((), (), s32[]{:S(2)}) async-start(), calls=%async_computation.15 | async-start | bytes 1048576 | tf_op jit(solution)/shard_map/while/body/eval_jaxpr/while/body/eval_jaxpr/psum | solution.py:103
  645.0 176.2 %all-gather.14.cloned.1.call-start = ((), (), s32[]{:S(2)}) async-start(), calls=%async_computation.17 | async-start | bytes 4456448 | tf_op jit(solution)/shard_map/while/body/eval_jaxpr/all_gather | solution.py:202
  645.6 209.7 %all-reduce.22.cloned.1.call-start = ((), (), s32[]{:S(2)}) async-start(), calls=%async_computation.18 | async-start | bytes 2097152 | tf_op jit(solution)/shard_map/while/body/eval_jaxpr/while/body/eval_jaxpr/psum | solution.py:130
  905.5 125.4 %all-gather.8.cloned.1.call-start = ((), (), s32[]{:S(2)}) async-start(), calls=%async_computation.13 | async-start | bytes 1114112 | tf_op jit(solution)/shard_map/while/body/eval_jaxpr/all_gather | solution.py:194
  906.1 181.7 %all-gather.10.cloned.1.call-start = ((), (), s32[]{:S(2)}) async-start(), calls=%async_computation.14 | async-start | bytes 1114112 | tf_op jit(solution)/shard_map/while/body/eval_jaxpr/all_gather | solution.py:201
  907.7 201.6 %all-reduce.20.cloned.1.call-start = ((), (), s32[]{:S(2)}) async-start(), calls=%async_computation.15 | async-start | bytes 1048576 | tf_op jit(solution)/shard_map/while/body/eval_jaxpr/while/body/eval_jaxpr/psum | solution.py:103
  1091.1 176.3 %all-gather.14.cloned.1.call-start = ((), (), s32[]{:S(2)}) async-start(), calls=%async_computation.17 | async-start | bytes 4456448 | tf_op jit(solution)/shard_map/while/body/eval_jaxpr/all_gather | solution.py:202
  1091.8 209.7 %all-reduce.22.cloned.1.call-start = ((), (), s32[]{:S(2)}) async-start(), calls=%async_computation.18 | async-start | bytes 2097152 | tf_op jit(solution)/shard_map/while/body/eval_jaxpr/while/body/eval_jaxpr/psum | solution.py:130
  1352.5 181.3 %all-gather.10.cloned.1.call-start = ((), (), s32[]{:S(2)}) async-start(), calls=%async_computation.14 | async-start | bytes 1114112 | tf_op jit(solution)/shard_map/while/body/eval_jaxpr/all_gather | solution.py:201
  1354.1 201.4 %all-reduce.20.cloned.1.call-start = ((), (), s32[]{:S(2)}) async-start(), calls=%async_computation.15 | async-start | bytes 1048576 | tf_op jit(solution)/shard_map/while/body/eval_jaxpr/while/body/eval_jaxpr/psum | solution.py:103
  1537.1 176.3 %all-gather.14.cloned.1.call-start = ((), (), s32[]{:S(2)}) async-start(), calls=%async_computation.17 | async-start | bytes 4456448 | tf_op jit(solution)/shard_map/while/body/eval_jaxpr/all_gather | solution.py:202
  1537.7 209.9 %all-reduce.22.cloned.1.call-start = ((), (), s32[]{:S(2)}) async-start(), calls=%async_computation.18 | async-start | bytes 2097152 | tf_op jit(solution)/shard_map/while/body/eval_jaxpr/while/body/eval_jaxpr/psum | solution.py:130
  1797.7 154.7 %reduce-scatter.9.cloned.1.call-start = ((), (), s32[]{:S(2)}) async-start(), calls=%async_computation.7 | async-start | bytes 2228224 | tf_op jit(solution)/shard_map/reduce_scatter | solution.py:233
  1798.3 235.0 %reduce-scatter.11.cloned.1.call-start = ((), (), s32[]{:S(2)}) async-start(), calls=%async_computation.8 | async-start | bytes 2228224 | tf_op jit(solution)/shard_map/reduce_scatter | solution.py:234
  1798.9 314.5 %reduce-scatter.13.cloned.1.call-start = ((), (), s32[]{:S(2)}) async-start(), calls=%async_computation.9 | async-start | bytes 2228224 | tf_op jit(solution)/shard_map/reduce_scatter | solution.py:241
  1801.3 502.7 %reduce-scatter.15.cloned.1.call-start = ((), (), s32[]{:S(2)}) async-start(), calls=%async_computation.10 | async-start | bytes 8912896 | tf_op jit(solution)/shard_map/reduce_scatter | solution.py:235
  1802.0 685.0 %reduce-scatter.17.cloned.1.call-start = ((), (), s32[]{:S(2)}) async-start(), calls=%async_computation.11 | async-start | bytes 8912896 | tf_op jit(solution)/shard_map/reduce_scatter | solution.py:242
  (161 other events, 2557.4 us)
Sparse Core Ops, SparseCore 0:
  17.0 66.6 all-gather.5
  86.4 54.0 all-gather.7
  143.3 54.0 all-gather.9
  222.0 76.9 all-gather.11
  302.0 74.6 all-gather.13
  431.3 19.8 all-reduce.23
  462.4 65.7 all-gather.5
  530.8 53.9 all-gather.7
  587.6 54.0 all-gather.9
  666.4 76.9 all-gather.11
  746.4 74.6 all-gather.13
  877.4 19.8 all-reduce.23
  908.2 66.0 all-gather.5
  976.9 53.9 all-gather.7
  1033.7 54.0 all-gather.9
  1112.5 76.9 all-gather.11
  1192.6 74.6 all-gather.13
  1323.6 19.8 all-reduce.23
  1354.8 65.6 all-gather.5
  1423.1 53.9 all-gather.7
  1479.7 54.0 all-gather.9
  1558.7 76.9 all-gather.11
  1638.7 74.6 all-gather.13
  1769.7 19.8 all-reduce.23
  (8 shorter events, 148.8 us)
Sparse Core Ops, SparseCore 1:
  1800.5 72.3 reduce-scatter.6
  1875.5 76.9 reduce-scatter.8
  1955.2 78.1 reduce-scatter.10
  2036.2 77.1 reduce-scatter.12
  2116.3 187.7 reduce-scatter.14
  2306.9 180.1 reduce-scatter.16
